TPU v7x, 32 devices: a whole 2x2x4 slice. The times are simulated.
32 devices in a mesh: grp: 2 (over x), col: 16 (over z, y, core).
Axes of the slice: x: 2, y: 2, z: 4, core: 2. Of those that a mesh axis runs over, the one named last changes fastest.
Arguments:
- mode_rows: float32 [16384, 256], P(('grp', 'col')), parts along dimension 0, may hold values from -8 to 8, as said below
- coeffs: bfloat16 [512, 256], P(('grp', 'col')), parts along dimension 0, may hold values from -18 to 18, as said below
- diffusivity: float32 [32, 64], P(('grp', 'col')), parts along dimension 0, may hold values from 0.02 to 0.24
- counts: int32 [32], P(('grp', 'col')), parts along dimension 0, may hold values from 32 to 64
- emis_idx: int32 [512], P('grp'), parts along dimension 0, may hold values from 0 to 15
- emis_table: float32 [16, 8], replicated, may hold values from 0.2 to 1.5
- reactants: int32 [12, 2], replicated, may hold values from 0 to 7
- stoich: int32 [12, 8], replicated, may hold values from -1 to 1
- rate_consts: float32 [12], replicated, may hold values from 0.02 to 0.2
- loss_rates: float32 [8], replicated, may hold values from 0.2 to 2
Outputs:
- modes_out: float32 [16384, 256], P(('grp', 'col')), parts along dimension 0
- coeffs_out: bfloat16 [512, 256], P(('grp', 'col')), parts along dimension 0
There are 2 independent parts, one for each index of `grp`. A program takes and returns all parts, laid end to end along the dimension named above; an argument that names none is the same for every part. Nothing has to cross between parts.
Inputs may be any that keep to these rules, and one draw needn't show every extreme that they name: `mode_rows`: modes of order one. `coeffs`: coefficients of order one.
All inputs are finite; a program needn't handle non-finite values.
Results may differ from a plain program's by a relative error of at most 0.0014.
The roundings to bfloat16 on the way count: a program that leaves them out, or rounds other values in their place, can miss the bound.
Values may be sent and summed in bfloat16 or wider, within the bound.
No kernel may reach another device: no remote copies, remote signals or barrier semaphores. Data moves between devices by JAX's collectives and lax.ppermute only.
A program may use at most 64 MiB of HBM per device.

v0:
```python
import math
import jax
import jax.numpy as jnp
from jax import lax
from jax.sharding import PartitionSpec as P

S = 8
LEV = 64
R = 256
NEMIS = 16
NSUB = 2
TIME_STEP = 0.1
RATE_STEP = 0.3
RIDGE_SHARE = 0.05
PRECISE = lax.Precision.HIGHEST


def diffuse(mode_block, diffusivity, counts):
    ncols = counts.shape[0]
    rank = mode_block.shape[1]
    blocked = mode_block.reshape(ncols, S, LEV, rank)
    level_index = jnp.arange(LEV, dtype=jnp.int32)
    face_coef = jnp.where(
        level_index[None, :] + 1 < counts[:, None], diffusivity, jnp.zeros_like(diffusivity)
    )
    upper_cells = jnp.concatenate([blocked[:, :, 1:], jnp.zeros_like(blocked[:, :, :1])], axis=2)
    face_flux = face_coef[:, None, :, None] * (upper_cells - blocked)
    lower_flux = jnp.concatenate(
        [jnp.zeros_like(face_flux[:, :, :1]), face_flux[:, :, :-1]], axis=2
    )
    return (blocked + face_flux - lower_flux).reshape(mode_block.shape)


def species_pick(table_column):
    return (table_column[:, None] == jnp.arange(S, dtype=jnp.int32)[None, :]).astype(jnp.float32)


def reaction(
    field_block,
    pick_first,
    pick_second,
    stoich_wide,
    rate_consts,
    loss_rates,
    emis_block,
    active,
    profile,
):
    first_amount = jnp.einsum("rs,bcsl->bcrl", pick_first, field_block, precision=PRECISE)
    second_amount = jnp.einsum("rs,bcsl->bcrl", pick_second, field_block, precision=PRECISE)
    reaction_speed = rate_consts[None, None, :, None] * first_amount * second_amount
    produced = jnp.einsum("rs,bcrl->bcsl", stoich_wide, reaction_speed, precision=PRECISE)
    tendency_raw = (
        produced
        - loss_rates[None, None, :, None] * field_block
        + emis_block[:, None, :, None] * profile[None, None, None, :]
    )
    return tendency_raw * active[None, :, None, :]


def on_device(
    mode_rows,
    coeffs,
    diffusivity,
    counts,
    emis_idx,
    emis_table,
    reactants,
    stoich,
    rate_consts,
    loss_rates,
):
    rows_dev = mode_rows.shape[0]
    mem_dev = coeffs.shape[0]
    col_count = lax.axis_size("col")
    total_rows = rows_dev * col_count
    members = mem_dev * col_count
    columns_dev = counts.shape[0]
    level_index = jnp.arange(LEV, dtype=jnp.int32)
    active = (level_index[None, :] < counts[:, None]).astype(jnp.float32)
    profile = jnp.exp(-4.0 * level_index.astype(jnp.float32) / LEV)
    chosen = (emis_idx[:, None] == jnp.arange(NEMIS, dtype=jnp.int32)[None, :]).astype(jnp.float32)
    member_emis = jnp.sum(chosen[:, :, None] * emis_table[None, :, :], axis=1)
    pick_first = species_pick(reactants[:, 0])
    pick_second = species_pick(reactants[:, 1])
    stoich_wide = stoich.astype(jnp.float32)
    rank_root = math.sqrt(R)
    inv_root = 1.0 / rank_root
    block_rows = math.gcd(members, 128)
    block_count = members // block_rows
    modes = mode_rows
    for substep in range(NSUB):
        diffused = diffuse(modes, diffusivity, counts)
        mode_bf = diffused.astype(jnp.bfloat16)
        rate_scale = rank_root / total_rows
        coef_gathered = lax.all_gather(coeffs, "col", axis=0, tiled=True)

        def member_block(pulled, block_inputs):
            coef_block, emis_block = block_inputs
            field_block = (
                lax.dot_general(
                    coef_block,
                    mode_bf,
                    (((1,), (1,)), ((), ())),
                    preferred_element_type=jnp.float32,
                )
                * inv_root
            )
            tendency = reaction(
                field_block.reshape(block_rows, columns_dev, S, LEV),
                pick_first,
                pick_second,
                stoich_wide,
                rate_consts,
                loss_rates,
                emis_block,
                active,
                profile,
            )
            tendency = tendency.reshape(block_rows, rows_dev).astype(jnp.bfloat16)
            pulled = pulled + lax.dot_general(
                tendency, coef_block, (((0,), (0,)), ((), ())), preferred_element_type=jnp.float32
            )
            part_rate = jnp.dot(tendency, mode_bf, preferred_element_type=jnp.float32)
            return (pulled, part_rate)

        pulled, rate_blocks = lax.scan(
            member_block,
            jnp.zeros((rows_dev, R), jnp.float32),
            (
                coef_gathered.reshape(block_count, block_rows, R),
                member_emis.reshape(block_count, block_rows, S),
            ),
        )
        pulled, rate_term = (pulled, rate_blocks.reshape(members, R))
        rate_mine = lax.psum_scatter(rate_term, "col", scatter_dimension=0, tiled=True) * rate_scale
        coef_wide = coeffs.astype(jnp.float32)
        gram_part = jnp.dot(coef_wide.T, coef_wide, precision=PRECISE)
        proj_part = lax.dot_general(
            mode_bf.astype(jnp.float32), pulled, (((0,), (0,)), ((), ())), precision=PRECISE
        )
        gram_matrix, proj_matrix = lax.psum((gram_part, proj_part), "col")
        proj_matrix = proj_matrix / total_rows
        gram_matrix = gram_matrix + RIDGE_SHARE * members * jnp.eye(R, dtype=jnp.float32)
        remainder = pulled - jnp.dot(diffused, proj_matrix, precision=PRECISE)
        factor = jnp.linalg.cholesky(gram_matrix)
        solved = jax.scipy.linalg.cho_solve((factor, True), remainder.T).T
        modes = diffused + TIME_STEP * rank_root * solved
        coeffs = (coef_wide + RATE_STEP * rate_mine).astype(jnp.bfloat16)
    return (modes, coeffs)


def solution(mesh):
    placed = (
        P(("grp", "col"), None),
        P(("grp", "col"), None),
        P(("grp", "col"), None),
        P(("grp", "col")),
        P("grp"),
        P(),
        P(),
        P(),
        P(),
        P(),
    )
    return jax.shard_map(
        on_device,
        mesh=mesh,
        in_specs=placed,
        out_specs=(P(("grp", "col"), None), P(("grp", "col"), None)),
        check_vma=False,
    )
```

profile of v0, /device:TPU:1, one launch (start us, length us, event | category | flops | bytes accessed | tf_op | source)
XLA Modules:
  0.0 393.6 jit_solution(5223242467514382098)
XLA Ops:
  7.2 23.6 %all_gather.6 = bf16[256,256]{1,0:T(8,128)(2,1)S(1)} all-gather(bf16[16,256]{1,0:T(8,128)(2,1)} %param.18), channel_id=1, replica_groups=mesh['grp'=2,'col'=16] {'col'}, dimensions={0}, use_global_device_ids=true | all-gather | bytes 139264 | tf_op jit(solution)/shard_map/all_gather | solution.py:96
  31.7 1.2 slice.80
  38.0 7.1 %while.30 = (s32[]{:T(128)}, f32[512,256]{1,0:T(8,128)S(1)}, f32[2,128,256]{2,1,0:T(8,128)S(1)}, f32[12]{0:T(128)S(1)}, bf16[2,128,256]{2,1,0:T(8,128)(2,1)S(1)}...) while((s32[]{:T(128)}, f32[512,256]{1,0:T(8,128)S(1)}, ...), condition=%wide.region_7.9_spmd.clone, body=%wide.region_6.8_spmd.clone.sunk | while | flops 129892992 | bytes 5650131 | solution.py:127
  45.1 1.2 fusion.103
  47.7 86.4 %all-reduce.12.cloned.1.call-done = (f32[256,256]{1,0:T(8,128)}, f32[256,256]{0,1:T(8,128)}) async-done(((f32[256,256]{1,0:T(8,128)}, f32[256,256]{0,1:T(8,128)}), (f32[256,256]{1,0:T(8,128)}, f32[256,256]{0,1:T(8,128)})) %all-reduce.12.cloned.1.call-update) | async-done | bytes 524304 | tf_op jit(solution)/shard_map/psum | solution.py:142
  136.1 11.7 %cholesky.130 = f32[128,128]{1,0:T(8,128)S(1)} custom-call(f32[128,128]{1,0:T(8,128)S(1)} %cholesky.194), custom_call_target="Cholesky" | custom-call | tf_op jit(solution)/shard_map/jit(cholesky)/cholesky | solution.py:146
  147.8 9.8 %custom-call.17 = f32[1,128,128]{1,2,0:T(8,128)S(1)} custom-call(f32[1,128,128]{2,1,0:T(8,128)S(1)} %get-tuple-element.369), custom_call_target="InvertDiagBlocksLowerTriangular" | custom-call | tf_op jit(solution)/shard_map/jit(cholesky)/cholesky | solution.py:146
  158.1 11.7 %cholesky.147 = f32[128,128]{1,0:T(8,128)S(1)} custom-call(f32[128,128]{1,0:T(8,128)S(1)} %convolution_subtract_fusion.7), custom_call_target="Cholesky" | custom-call | tf_op jit(solution)/shard_map/jit(cholesky)/cholesky | solution.py:146
  171.9 4.4 %while.32 = (s32[]{:T(128)}, f32[256,256]{1,0:T(8,128)S(1)}, s32[2,2]{1,0:T(2,128)S(1)}, f32[2,128,128]{2,1,0:T(8,128)S(1)}, s32[]{:T(128)}) while((s32[]{:T(128)}, f32[256,256]{1,0:T(8,128)S(1)}, s32[2,2]{1,0:T(2,128)S(1)}, f32[2,128,128]{2,1,0:T(8,128)S(1)}, s32[]{:T(128)}) %tuple.90), condition=%wide.while_cond, body=%wide.while_body.sunk | while | flops 2 | bytes 131181 | solution.py:147
  173.0 1.3 bitcast_dynamic-update-slice_fusion.4
  174.9 1.3 bitcast_dynamic-update-slice_fusion.4
  176.2 19.7 %custom-call.18 = f32[2,128,128]{1,2,0:T(8,128)S(1)} custom-call(f32[2,128,128]{2,1,0:T(8,128)S(1)} %get-tuple-element.258), custom_call_target="InvertDiagBlocksLowerTriangular" | custom-call | tf_op jit(solution)/shard_map/jit(_cho_solve)/triangular_solve | solution.py:147
  200.6 21.0 %all_gather.7 = bf16[256,256]{1,0:T(8,128)(2,1)S(1)} all-gather(bf16[16,256]{1,0:T(8,128)(2,1)S(1)} %add_convert_fusion.1), channel_id=1, replica_groups=mesh['grp'=2,'col'=16] {'col'}, dimensions={0}, use_global_device_ids=true | all-gather | bytes 139264 | tf_op jit(solution)/shard_map/all_gather | solution.py:96
  222.6 7.1 %while.31 = (s32[]{:T(128)}, f32[512,256]{1,0:T(8,128)S(1)}, f32[2,128,256]{2,1,0:T(8,128)S(1)}, f32[12]{0:T(128)S(1)}, bf16[2,128,256]{2,1,0:T(8,128)(2,1)S(1)}...) while((s32[]{:T(128)}, f32[512,256]{1,0:T(8,128)S(1)}, ...), condition=%wide.region_12.15_spmd.clone, body=%wide.region_11.14_spmd.clone.sunk | while | flops 129892992 | bytes 5650131 | solution.py:127
  229.7 1.2 fusion.105
  231.5 87.1 %all-reduce.10.cloned.1.call-done = (f32[256,256]{1,0:T(8,128)}, f32[256,256]{0,1:T(8,128)}) async-done(((f32[256,256]{1,0:T(8,128)}, f32[256,256]{0,1:T(8,128)}), (f32[256,256]{1,0:T(8,128)}, f32[256,256]{0,1:T(8,128)})) %all-reduce.10.cloned.1.call-update) | async-done | bytes 524304 | tf_op jit(solution)/shard_map/psum | solution.py:142
  320.6 11.7 %cholesky.164 = f32[128,128]{1,0:T(8,128)S(1)} custom-call(f32[128,128]{1,0:T(8,128)S(1)} %cholesky.197), custom_call_target="Cholesky" | custom-call | tf_op jit(solution)/shard_map/jit(cholesky)/cholesky | solution.py:146
  332.4 9.8 %custom-call.19 = f32[1,128,128]{1,2,0:T(8,128)S(1)} custom-call(f32[1,128,128]{2,1,0:T(8,128)S(1)} %get-tuple-element.365), custom_call_target="InvertDiagBlocksLowerTriangular" | custom-call | tf_op jit(solution)/shard_map/jit(cholesky)/cholesky | solution.py:146
  342.7 11.7 %cholesky.181 = f32[128,128]{1,0:T(8,128)S(1)} custom-call(f32[128,128]{1,0:T(8,128)S(1)} %convolution_subtract_fusion.6), custom_call_target="Cholesky" | custom-call | tf_op jit(solution)/shard_map/jit(cholesky)/cholesky | solution.py:146
  357.2 4.3 %while.33 = (s32[]{:T(128)}, f32[256,256]{1,0:T(8,128)S(1)}, s32[2,2]{1,0:T(2,128)S(1)}, f32[2,128,128]{2,1,0:T(8,128)S(1)}, s32[]{:T(128)}) while((s32[]{:T(128)}, f32[256,256]{1,0:T(8,128)S(1)}, s32[2,2]{1,0:T(2,128)S(1)}, f32[2,128,128]{2,1,0:T(8,128)S(1)}, s32[]{:T(128)}) %tuple.120), condition=%wide.while_cond.clone, body=%wide.while_body.clone.sunk | while | flops 2 | bytes 131181 | solution.py:147
  358.0 1.4 bitcast_dynamic-update-slice_fusion.5
  360.1 1.4 bitcast_dynamic-update-slice_fusion.5
  361.5 19.7 %custom-call.20 = f32[2,128,128]{1,2,0:T(8,128)S(1)} custom-call(f32[2,128,128]{2,1,0:T(8,128)S(1)} %get-tuple-element.259), custom_call_target="InvertDiagBlocksLowerTriangular" | custom-call | tf_op jit(solution)/shard_map/jit(_cho_solve)/triangular_solve | solution.py:147
  385.5 1.3 add_convert_fusion
  (159 shorter events, 40.4 us)
Async XLA Ops:
  7.2 126.9 %all-reduce.12.cloned.1.call-start = ((), (), s32[]{:S(2)}) async-start(), calls=%async_computation.5 | async-start | bytes 1048576 | tf_op jit(solution)/shard_map/psum | solution.py:142
  7.2 23.6 %copy-start.7 = (bf16[16,256]{1,0:T(8,128)(2,1)S(1)}, bf16[16,256]{1,0:T(8,128)(2,1)}, u32[]{:S(2)}) copy-start(bf16[16,256]{1,0:T(8,128)(2,1)} %param.18) | copy-start | bytes 24580
  31.7 2.5 copy-start
  33.6 0.7 copy-start.14
  34.5 0.7 copy-start.13
  35.2 0.7 copy-start.12
  35.9 0.7 copy-start.10
  36.6 0.7 copy-start.11
  37.4 0.7 copy-start.8
  37.4 0.7 copy-start.9
  45.1 1.2 copy-start.3
  46.3 153.5 %reduce-scatter.3.cloned.1.call-start = ((), (), s32[]{:S(2)}) async-start(), calls=%async_computation.2 | async-start | bytes 278528 | tf_op jit(solution)/shard_map/reduce_scatter | solution.py:136
  47.1 271.5 %all-reduce.10.cloned.1.call-start = ((), (), s32[]{:S(2)}) async-start(), calls=%async_computation.4 | async-start | bytes 1048576 | tf_op jit(solution)/shard_map/psum | solution.py:142
  135.1 1.0 copy-start.1
  171.9 24.1 %copy-start.5 = (f32[256,256]{1,0:T(8,128)S(1)}, f32[256,256]{1,0:T(8,128)}, u32[]{:S(2)}) copy-start(f32[256,256]{1,0:T(8,128)} %get-tuple-element.356) | copy-start | bytes 786436
  229.7 1.2 copy-start.4
  230.9 154.6 %reduce-scatter.5.cloned.1.call-start = ((), (), s32[]{:S(2)}) async-start(), calls=%async_computation.3 | async-start | bytes 278528 | tf_op jit(solution)/shard_map/reduce_scatter | solution.py:136
  319.6 1.0 copy-start.2
  357.2 24.0 %copy-start.6 = (f32[256,256]{1,0:T(8,128)S(1)}, f32[256,256]{1,0:T(8,128)}, u32[]{:S(2)}) copy-start(f32[256,256]{1,0:T(8,128)} %get-tuple-element.354) | copy-start | bytes 786436
Sparse Core Ops, SparseCore 0:
  46.5 87.5 all-reduce.11
  137.6 53.6 reduce-scatter.2
  231.0 87.5 all-reduce.9
  322.0 53.5 reduce-scatter.4
where the time goes:
time: 398 us; the launch traced here: 394 us
  waiting for transfers between devices  174 us (44%)
  other arithmetic  116 us (29%)
  blocking collectives  44.6 us (11%)
  matrix products  22 us (6%)
  between operations  17.7 us (4%)
  local copies, waits for them, and re-layouts  17.3 us (4%)
    psum x2, waiting for transfers between devices, on_device(): gram_matrix, proj_matrix = lax.psum((gram_part, proj_part), 'col')  174 us
    another operation x13, other arithmetic, on_device(): factor = jnp.linalg.cholesky(gram_matrix)  68.6 us
    all_gather x2, blocking collectives, on_device(): coef_gathered = lax.all_gather(coeffs, 'col', axis=0, tiled=True)  44.6 us
    another operation x5, other arithmetic, on_device(): solved = jax.scipy.linalg.cho_solve((factor, True), remainder.T).T  39.4 us
  transfers between devices with their start and end apart: 4, of which 2 were waited for; matrix products, arithmetic and copies ran while one was open for 32% of the time, Pallas kernels for 0%

commit v1 on v0

--- a/solution.py
+++ b/solution.py
@@ -13,6 +13,23 @@
 RATE_STEP = 0.3
 RIDGE_SHARE = 0.05
 PRECISE = lax.Precision.HIGHEST
+
+
+def launch_loops(x_in, where_dim):
+    n_shards = lax.axis_size("col")
+    rack = []
+    for tick in range(1, n_shards):
+        rack.append((tick - 1, tick))
+    t_next = rack + [(n_shards - 1, 0)]
+    right_arr = x_in
+    copies = [right_arr]
+    for _ in range(n_shards - 1):
+        right_arr = lax.ppermute(right_arr, "col", t_next)
+        copies += [right_arr]
+    x_next = jnp.concatenate([*reversed(copies)], axis=where_dim)
+    return jnp.roll(
+        x_next, (lax.axis_index("col") + 1) * right_arr.shape[where_dim], axis=where_dim
+    )
 
 
 def diffuse(mode_block, diffusivity, counts):
@@ -93,7 +110,7 @@
         diffused = diffuse(modes, diffusivity, counts)
         mode_bf = diffused.astype(jnp.bfloat16)
         rate_scale = rank_root / total_rows
-        coef_gathered = lax.all_gather(coeffs, "col", axis=0, tiled=True)
+        coef_gathered = launch_loops(coeffs, 0)
 
         def member_block(pulled, block_inputs):
             coef_block, emis_block = block_inputs

time: 398 us -> 531 us (1.33)
  waiting for transfers between devices: 174 us -> 338 us
  blocking collectives: 44.6 us -> 0 us
  starting transfers between devices: 0.62 us -> 15.3 us
    ppermute x0 -> x30, waiting for transfers between devices: none -> 133 us  [launch_loops(): right_arr = lax.ppermute(right_arr, 'col', t_next)]
    all_gather x2 -> x0, blocking collectives: 44.6 us -> none  [on_device(): coef_gathered = lax.all_gather(coeffs, 'col', axis=0, tiled=True)]
    reduce_scatter x2, waiting for transfers between devices: 0.02 us -> 21.2 us  [on_device(): lax.psum_scatter(rate_term, 'col', scatter_dimension=0, tiled=True)]
    ppermute x0 -> x30, starting transfers between devices: none -> 14.4 us  [launch_loops(): right_arr = lax.ppermute(right_arr, 'col', t_next)]
    psum x2, waiting for transfers between devices: 174 us -> 184 us  [on_device(): gram_matrix, proj_matrix = lax.psum((gram_part, proj_part), 'col')]
  transfers between devices with their start and end apart: 4 -> 34, of which waited for: 2 -> 31; matrix products, arithmetic and copies ran while one was open for 32% -> 25% of each run, Pallas kernels for 0% -> 0%
where the time goes in v1:
time: 531 us; the launch traced here: 526 us
  waiting for transfers between devices  338 us (64%)
  other arithmetic  116 us (22%)
  matrix products  22 us (4%)
  between operations  18.1 us (3%)
  starting transfers between devices  15.3 us (3%)
  local copies, waits for them, and re-layouts  14.9 us (3%)
    psum x2, waiting for transfers between devices, on_device(): gram_matrix, proj_matrix = lax.psum((gram_part, proj_part), 'col')  184 us
    ppermute x30, waiting for transfers between devices, launch_loops(): right_arr = lax.ppermute(right_arr, 'col', t_next)  133 us
    another operation x13, other arithmetic, on_device(): factor = jnp.linalg.cholesky(gram_matrix)  68.6 us
    another operation x5, other arithmetic, on_device(): solved = jax.scipy.linalg.cho_solve((factor, True), remainder.T).T  39.4 us
    reduce_scatter x2, waiting for transfers between devices, on_device(): lax.psum_scatter(rate_term, 'col', scatter_dimension=0, tiled=True)  21.2 us
    ppermute x30, starting transfers between devices, launch_loops(): right_arr = lax.ppermute(right_arr, 'col', t_next)  14.4 us
  transfers between devices with their start and end apart: 34, of which 31 were waited for; matrix products, arithmetic and copies ran while one was open for 25% of the time, Pallas kernels for 0%

profile of v1, /device:TPU:1, one launch (start us, length us, event | category | flops | bytes accessed | tf_op | source)
XLA Modules:
  0.0 525.5 jit_solution(13208743976788440913)
XLA Ops:
  20.8 5.8 %collective-permute-done.3 = bf16[16,256]{1,0:T(8,128)(2,1)S(1)} collective-permute-done((bf16[16,256]{1,0:T(8,128)(2,1)S(1)}, bf16[16,256]{1,0:T(8,128)(2,1)S(1)}, u32[]{:S(2)}, u32[]{:S(2)}) %collective-permute-start.3) | collective-permute-done | bytes 8224 | tf_op jit(solution)/shard_map/ppermute | solution.py:27
  26.5 5.8 %collective-permute-done.4 = bf16[16,256]{1,0:T(8,128)(2,1)S(1)} collective-permute-done((bf16[16,256]{1,0:T(8,128)(2,1)S(1)}, bf16[16,256]{1,0:T(8,128)(2,1)S(1)}, u32[]{:S(2)}, u32[]{:S(2)}) %collective-permute-start.4) | collective-permute-done | bytes 8224 | tf_op jit(solution)/shard_map/ppermute | solution.py:27
  32.3 5.8 %collective-permute-done.5 = bf16[16,256]{1,0:T(8,128)(2,1)S(1)} collective-permute-done((bf16[16,256]{1,0:T(8,128)(2,1)S(1)}, bf16[16,256]{1,0:T(8,128)(2,1)S(1)}, u32[]{:S(2)}, u32[]{:S(2)}) %collective-permute-start.5) | collective-permute-done | bytes 8224 | tf_op jit(solution)/shard_map/ppermute | solution.py:27
  49.8 5.6 %collective-permute-done.8 = bf16[16,256]{1,0:T(8,128)(2,1)S(1)} collective-permute-done((bf16[16,256]{1,0:T(8,128)(2,1)S(1)}, bf16[16,256]{1,0:T(8,128)(2,1)S(1)}, u32[]{:S(2)}, u32[]{:S(2)}) %collective-permute-start.8) | collective-permute-done | bytes 8224 | tf_op jit(solution)/shard_map/ppermute | solution.py:27
  55.5 5.7 %collective-permute-done.9 = bf16[16,256]{1,0:T(8,128)(2,1)S(1)} collective-permute-done((bf16[16,256]{1,0:T(8,128)(2,1)S(1)}, bf16[16,256]{1,0:T(8,128)(2,1)S(1)}, u32[]{:S(2)}, u32[]{:S(2)}) %collective-permute-start.9) | collective-permute-done | bytes 8224 | tf_op jit(solution)/shard_map/ppermute | solution.py:27
  61.2 5.7 %collective-permute-done.10 = bf16[16,256]{1,0:T(8,128)(2,1)S(1)} collective-permute-done((bf16[16,256]{1,0:T(8,128)(2,1)S(1)}, bf16[16,256]{1,0:T(8,128)(2,1)S(1)}, u32[]{:S(2)}, u32[]{:S(2)}) %collective-permute-start.10) | collective-permute-done | bytes 8224 | tf_op jit(solution)/shard_map/ppermute | solution.py:27
  72.7 5.7 %collective-permute-done.12 = bf16[16,256]{1,0:T(8,128)(2,1)S(1)} collective-permute-done((bf16[16,256]{1,0:T(8,128)(2,1)S(1)}, bf16[16,256]{1,0:T(8,128)(2,1)S(1)}, u32[]{:S(2)}, u32[]{:S(2)}) %collective-permute-start.12) | collective-permute-done | bytes 8224 | tf_op jit(solution)/shard_map/ppermute | solution.py:27
  78.6 5.7 %collective-permute-done.13 = bf16[16,256]{1,0:T(8,128)(2,1)S(1)} collective-permute-done((bf16[16,256]{1,0:T(8,128)(2,1)S(1)}, bf16[16,256]{1,0:T(8,128)(2,1)S(1)}, u32[]{:S(2)}, u32[]{:S(2)}) %collective-permute-start.13) | collective-permute-done | bytes 8224 | tf_op jit(solution)/shard_map/ppermute | solution.py:27
  91.2 7.1 %while.30 = (s32[]{:T(128)}, f32[512,256]{1,0:T(8,128)S(1)}, f32[2,128,256]{2,1,0:T(8,128)S(1)}, f32[12]{0:T(128)S(1)}, bf16[2,128,256]{2,1,0:T(8,128)(2,1)S(1)}...) while((s32[]{:T(128)}, f32[512,256]{1,0:T(8,128)S(1)}, ...), condition=%wide.region_7.10_spmd.clone, body=%wide.region_6.9_spmd.clone.sunk | while | flops 129892992 | bytes 5650131 | solution.py:144
  100.8 91.8 %all-reduce.12.cloned.1.call-done = (f32[256,256]{1,0:T(8,128)}, f32[256,256]{0,1:T(8,128)}) async-done(((f32[256,256]{1,0:T(8,128)}, f32[256,256]{0,1:T(8,128)}), (f32[256,256]{1,0:T(8,128)}, f32[256,256]{0,1:T(8,128)})) %all-reduce.12.cloned.1.call-update) | async-done | bytes 524304 | tf_op jit(solution)/shard_map/psum | solution.py:159
  194.5 11.7 %cholesky.130 = f32[128,128]{1,0:T(8,128)S(1)} custom-call(f32[128,128]{1,0:T(8,128)S(1)} %cholesky.194), custom_call_target="Cholesky" | custom-call | tf_op jit(solution)/shard_map/jit(cholesky)/cholesky | solution.py:163
  206.3 9.8 %custom-call.17 = f32[1,128,128]{1,2,0:T(8,128)S(1)} custom-call(f32[1,128,128]{2,1,0:T(8,128)S(1)} %get-tuple-element.370), custom_call_target="InvertDiagBlocksLowerTriangular" | custom-call | tf_op jit(solution)/shard_map/jit(cholesky)/cholesky | solution.py:163
  216.6 11.7 %cholesky.147 = f32[128,128]{1,0:T(8,128)S(1)} custom-call(f32[128,128]{1,0:T(8,128)S(1)} %convolution_subtract_fusion.7), custom_call_target="Cholesky" | custom-call | tf_op jit(solution)/shard_map/jit(cholesky)/cholesky | solution.py:163
  228.4 21.2 %reduce-scatter.3.cloned.1.call-done = f32[16,256]{1,0:T(8,128)} async-done(((f32[256,256]{1,0:T(8,128)}), f32[16,256]{1,0:T(8,128)}) %reduce-scatter.3.cloned.1.call-update) | async-done | bytes 16400 | tf_op jit(solution)/shard_map/reduce_scatter | solution.py:153
  265.9 19.7 %custom-call.18 = f32[2,128,128]{1,2,0:T(8,128)S(1)} custom-call(f32[2,128,128]{2,1,0:T(8,128)S(1)} %get-tuple-element.259), custom_call_target="InvertDiagBlocksLowerTriangular" | custom-call | tf_op jit(solution)/shard_map/jit(_cho_solve)/triangular_solve | solution.py:164
  326.2 5.6 %collective-permute-done.26 = bf16[16,256]{1,0:T(8,128)(2,1)S(1)} collective-permute-done((bf16[16,256]{1,0:T(8,128)(2,1)S(1)}, bf16[16,256]{1,0:T(8,128)(2,1)S(1)}, u32[]{:S(2)}, u32[]{:S(2)}) %collective-permute-start.26) | collective-permute-done | bytes 8224 | tf_op jit(solution)/shard_map/ppermute | solution.py:27
  331.9 5.7 %collective-permute-done.27 = bf16[16,256]{1,0:T(8,128)(2,1)S(1)} collective-permute-done((bf16[16,256]{1,0:T(8,128)(2,1)S(1)}, bf16[16,256]{1,0:T(8,128)(2,1)S(1)}, u32[]{:S(2)}, u32[]{:S(2)}) %collective-permute-start.27) | collective-permute-done | bytes 8224 | tf_op jit(solution)/shard_map/ppermute | solution.py:27
  337.6 5.7 %collective-permute-done.28 = bf16[16,256]{1,0:T(8,128)(2,1)S(1)} collective-permute-done((bf16[16,256]{1,0:T(8,128)(2,1)S(1)}, bf16[16,256]{1,0:T(8,128)(2,1)S(1)}, u32[]{:S(2)}, u32[]{:S(2)}) %collective-permute-start.28) | collective-permute-done | bytes 8224 | tf_op jit(solution)/shard_map/ppermute | solution.py:27
  349.6 7.1 %while.31 = (s32[]{:T(128)}, f32[512,256]{1,0:T(8,128)S(1)}, f32[2,128,256]{2,1,0:T(8,128)S(1)}, f32[12]{0:T(128)S(1)}, bf16[2,128,256]{2,1,0:T(8,128)(2,1)S(1)}...) while((s32[]{:T(128)}, f32[512,256]{1,0:T(8,128)S(1)}, ...), condition=%wide.region_12.16_spmd.clone, body=%wide.region_11.15_spmd.clone.sunk | while | flops 129892992 | bytes 5650131 | solution.py:144
  358.5 92.0 %all-reduce.10.cloned.1.call-done = (f32[256,256]{1,0:T(8,128)}, f32[256,256]{0,1:T(8,128)}) async-done(((f32[256,256]{1,0:T(8,128)}, f32[256,256]{0,1:T(8,128)}), (f32[256,256]{1,0:T(8,128)}, f32[256,256]{0,1:T(8,128)})) %all-reduce.10.cloned.1.call-update) | async-done | bytes 524304 | tf_op jit(solution)/shard_map/psum | solution.py:159
  452.5 11.7 %cholesky.164 = f32[128,128]{1,0:T(8,128)S(1)} custom-call(f32[128,128]{1,0:T(8,128)S(1)} %cholesky.197), custom_call_target="Cholesky" | custom-call | tf_op jit(solution)/shard_map/jit(cholesky)/cholesky | solution.py:163
  464.3 9.8 %custom-call.19 = f32[1,128,128]{1,2,0:T(8,128)S(1)} custom-call(f32[1,128,128]{2,1,0:T(8,128)S(1)} %get-tuple-element.366), custom_call_target="InvertDiagBlocksLowerTriangular" | custom-call | tf_op jit(solution)/shard_map/jit(cholesky)/cholesky | solution.py:163
  474.6 11.7 %cholesky.181 = f32[128,128]{1,0:T(8,128)S(1)} custom-call(f32[128,128]{1,0:T(8,128)S(1)} %convolution_subtract_fusion.6), custom_call_target="Cholesky" | custom-call | tf_op jit(solution)/shard_map/jit(cholesky)/cholesky | solution.py:163
  493.4 19.7 %custom-call.20 = f32[2,128,128]{1,2,0:T(8,128)S(1)} custom-call(f32[2,128,128]{2,1,0:T(8,128)S(1)} %get-tuple-element.260), custom_call_target="InvertDiagBlocksLowerTriangular" | custom-call | tf_op jit(solution)/shard_map/jit(_cho_solve)/triangular_solve | solution.py:164
  (251 shorter events, 141.4 us)
Async XLA Ops:
  7.2 185.4 %all-reduce.12.cloned.1.call-start = ((), (), s32[]{:S(2)}) async-start(), calls=%async_computation.5 | async-start | bytes 1048576 | tf_op jit(solution)/shard_map/psum | solution.py:159
  15.0 5.8 %collective-permute-start.2 = (bf16[16,256]{1,0:T(8,128)(2,1)S(1)}, bf16[16,256]{1,0:T(8,128)(2,1)S(1)}, u32[]{:S(2)}, u32[]{:S(2)}) collective-permute-start(bf16[16,256]{1,0:T(8,128)(2,1)S(1)} %collective-permute-done.1), channel_id=1, source_target_pairs={{0,1},{1,2},{2,3},{3,4},{4,5},{5,6},{6,7},{7,8},{8,9},{9,10},{10,1... | collective-permute-start | bytes 24584 | tf_op jit(solution)/shard_map/ppermute | solution.py:27
  20.8 5.8 %collective-permute-start.3 = (bf16[16,256]{1,0:T(8,128)(2,1)S(1)}, bf16[16,256]{1,0:T(8,128)(2,1)S(1)}, u32[]{:S(2)}, u32[]{:S(2)}) collective-permute-start(bf16[16,256]{1,0:T(8,128)(2,1)S(1)} %collective-permute-done.2), channel_id=1, source_target_pairs={{0,1},{1,2},{2,3},{3,4},{4,5},{5,6},{6,7},{7,8},{8,9},{9,10},{10,1... | collective-permute-start | bytes 24584 | tf_op jit(solution)/shard_map/ppermute | solution.py:27
  26.5 5.8 %collective-permute-start.4 = (bf16[16,256]{1,0:T(8,128)(2,1)S(1)}, bf16[16,256]{1,0:T(8,128)(2,1)S(1)}, u32[]{:S(2)}, u32[]{:S(2)}) collective-permute-start(bf16[16,256]{1,0:T(8,128)(2,1)S(1)} %collective-permute-done.3), channel_id=1, source_target_pairs={{0,1},{1,2},{2,3},{3,4},{4,5},{5,6},{6,7},{7,8},{8,9},{9,10},{10,1... | collective-permute-start | bytes 24584 | tf_op jit(solution)/shard_map/ppermute | solution.py:27
  32.3 5.8 %collective-permute-start.5 = (bf16[16,256]{1,0:T(8,128)(2,1)S(1)}, bf16[16,256]{1,0:T(8,128)(2,1)S(1)}, u32[]{:S(2)}, u32[]{:S(2)}) collective-permute-start(bf16[16,256]{1,0:T(8,128)(2,1)S(1)} %collective-permute-done.4), channel_id=1, source_target_pairs={{0,1},{1,2},{2,3},{3,4},{4,5},{5,6},{6,7},{7,8},{8,9},{9,10},{10,1... | collective-permute-start | bytes 24584 | tf_op jit(solution)/shard_map/ppermute | solution.py:27
  38.1 5.8 %collective-permute-start.6 = (bf16[16,256]{1,0:T(8,128)(2,1)S(1)}, bf16[16,256]{1,0:T(8,128)(2,1)S(1)}, u32[]{:S(2)}, u32[]{:S(2)}) collective-permute-start(bf16[16,256]{1,0:T(8,128)(2,1)S(1)} %collective-permute-done.5), channel_id=1, source_target_pairs={{0,1},{1,2},{2,3},{3,4},{4,5},{5,6},{6,7},{7,8},{8,9},{9,10},{10,1... | collective-permute-start | bytes 24584 | tf_op jit(solution)/shard_map/ppermute | solution.py:27
  43.8 5.8 %collective-permute-start.7 = (bf16[16,256]{1,0:T(8,128)(2,1)S(1)}, bf16[16,256]{1,0:T(8,128)(2,1)S(1)}, u32[]{:S(2)}, u32[]{:S(2)}) collective-permute-start(bf16[16,256]{1,0:T(8,128)(2,1)S(1)} %collective-permute-done.6), channel_id=1, source_target_pairs={{0,1},{1,2},{2,3},{3,4},{4,5},{5,6},{6,7},{7,8},{8,9},{9,10},{10,1... | collective-permute-start | bytes 24584 | tf_op jit(solution)/shard_map/ppermute | solution.py:27
  49.6 5.8 %collective-permute-start.8 = (bf16[16,256]{1,0:T(8,128)(2,1)S(1)}, bf16[16,256]{1,0:T(8,128)(2,1)S(1)}, u32[]{:S(2)}, u32[]{:S(2)}) collective-permute-start(bf16[16,256]{1,0:T(8,128)(2,1)S(1)} %collective-permute-done.7), channel_id=1, source_target_pairs={{0,1},{1,2},{2,3},{3,4},{4,5},{5,6},{6,7},{7,8},{8,9},{9,10},{10,1... | collective-permute-start | bytes 24584 | tf_op jit(solution)/shard_map/ppermute | solution.py:27
  55.4 5.8 %collective-permute-start.9 = (bf16[16,256]{1,0:T(8,128)(2,1)S(1)}, bf16[16,256]{1,0:T(8,128)(2,1)S(1)}, u32[]{:S(2)}, u32[]{:S(2)}) collective-permute-start(bf16[16,256]{1,0:T(8,128)(2,1)S(1)} %collective-permute-done.8), channel_id=1, source_target_pairs={{0,1},{1,2},{2,3},{3,4},{4,5},{5,6},{6,7},{7,8},{8,9},{9,10},{10,1... | collective-permute-start | bytes 24584 | tf_op jit(solution)/shard_map/ppermute | solution.py:27
  61.2 5.8 %collective-permute-start.10 = (bf16[16,256]{1,0:T(8,128)(2,1)S(1)}, bf16[16,256]{1,0:T(8,128)(2,1)S(1)}, u32[]{:S(2)}, u32[]{:S(2)}) collective-permute-start(bf16[16,256]{1,0:T(8,128)(2,1)S(1)} %collective-permute-done.9), channel_id=1, source_target_pairs={{0,1},{1,2},{2,3},{3,4},{4,5},{5,6},{6,7},{7,8},{8,9},{9,10},{10,1... | collective-permute-start | bytes 24584 | tf_op jit(solution)/shard_map/ppermute | solution.py:27
  66.9 5.8 %collective-permute-start.11 = (bf16[16,256]{1,0:T(8,128)(2,1)S(1)}, bf16[16,256]{1,0:T(8,128)(2,1)S(1)}, u32[]{:S(2)}, u32[]{:S(2)}) collective-permute-start(bf16[16,256]{1,0:T(8,128)(2,1)S(1)} %collective-permute-done.10), channel_id=1, source_target_pairs={{0,1},{1,2},{2,3},{3,4},{4,5},{5,6},{6,7},{7,8},{8,9},{9,10},{10,1... | collective-permute-start | bytes 24584 | tf_op jit(solution)/shard_map/ppermute | solution.py:27
  72.7 5.8 %collective-permute-start.12 = (bf16[16,256]{1,0:T(8,128)(2,1)S(1)}, bf16[16,256]{1,0:T(8,128)(2,1)S(1)}, u32[]{:S(2)}, u32[]{:S(2)}) collective-permute-start(bf16[16,256]{1,0:T(8,128)(2,1)S(1)} %collective-permute-done.11), channel_id=1, source_target_pairs={{0,1},{1,2},{2,3},{3,4},{4,5},{5,6},{6,7},{7,8},{8,9},{9,10},{10,1... | collective-permute-start | bytes 24584 | tf_op jit(solution)/shard_map/ppermute | solution.py:27
  78.5 5.8 %collective-permute-start.13 = (bf16[16,256]{1,0:T(8,128)(2,1)S(1)}, bf16[16,256]{1,0:T(8,128)(2,1)S(1)}, u32[]{:S(2)}, u32[]{:S(2)}) collective-permute-start(bf16[16,256]{1,0:T(8,128)(2,1)S(1)} %collective-permute-done.12), channel_id=1, source_target_pairs={{0,1},{1,2},{2,3},{3,4},{4,5},{5,6},{6,7},{7,8},{8,9},{9,10},{10,1... | collective-permute-start | bytes 24584 | tf_op jit(solution)/shard_map/ppermute | solution.py:27
  84.3 5.8 %collective-permute-start.14 = (bf16[16,256]{1,0:T(8,128)(2,1)S(1)}, bf16[16,256]{1,0:T(8,128)(2,1)S(1)}, u32[]{:S(2)}, u32[]{:S(2)}) collective-permute-start(bf16[16,256]{1,0:T(8,128)(2,1)S(1)} %collective-permute-done.13), channel_id=1, source_target_pairs={{0,1},{1,2},{2,3},{3,4},{4,5},{5,6},{6,7},{7,8},{8,9},{9,10},{10,1... | collective-permute-start | bytes 24584 | tf_op jit(solution)/shard_map/ppermute | solution.py:27
  99.5 150.1 %reduce-scatter.3.cloned.1.call-start = ((), (), s32[]{:S(2)}) async-start(), calls=%async_computation.2 | async-start | bytes 278528 | tf_op jit(solution)/shard_map/reduce_scatter | solution.py:153
  100.2 350.3 %all-reduce.10.cloned.1.call-start = ((), (), s32[]{:S(2)}) async-start(), calls=%async_computation.4 | async-start | bytes 1048576 | tf_op jit(solution)/shard_map/psum | solution.py:159
  259.3 5.8 %collective-permute-start.17 = (bf16[16,256]{1,0:T(8,128)(2,1)S(1)}, bf16[16,256]{1,0:T(8,128)(2,1)S(1)}, u32[]{:S(2)}, u32[]{:S(2)}) collective-permute-start(bf16[16,256]{1,0:T(8,128)(2,1)S(1)} %collective-permute-done.16), channel_id=1, source_target_pairs={{0,1},{1,2},{2,3},{3,4},{4,5},{5,6},{6,7},{7,8},{8,9},{9,10},{10,1... | collective-permute-start | bytes 24584 | tf_op jit(solution)/shard_map/ppermute | solution.py:27
  265.1 20.5 %collective-permute-start.18 = (bf16[16,256]{1,0:T(8,128)(2,1)S(1)}, bf16[16,256]{1,0:T(8,128)(2,1)S(1)}, u32[]{:S(2)}, u32[]{:S(2)}) collective-permute-start(bf16[16,256]{1,0:T(8,128)(2,1)S(1)} %collective-permute-done.17), channel_id=1, source_target_pairs={{0,1},{1,2},{2,3},{3,4},{4,5},{5,6},{6,7},{7,8},{8,9},{9,10},{10,1... | collective-permute-start | bytes 24584 | tf_op jit(solution)/shard_map/ppermute | solution.py:27
  285.6 5.8 %collective-permute-start.19 = (bf16[16,256]{1,0:T(8,128)(2,1)S(1)}, bf16[16,256]{1,0:T(8,128)(2,1)S(1)}, u32[]{:S(2)}, u32[]{:S(2)}) collective-permute-start(bf16[16,256]{1,0:T(8,128)(2,1)S(1)} %collective-permute-done.18), channel_id=1, source_target_pairs={{0,1},{1,2},{2,3},{3,4},{4,5},{5,6},{6,7},{7,8},{8,9},{9,10},{10,1... | collective-permute-start | bytes 24584 | tf_op jit(solution)/shard_map/ppermute | solution.py:27
  297.2 5.8 %collective-permute-start.21 = (bf16[16,256]{1,0:T(8,128)(2,1)S(1)}, bf16[16,256]{1,0:T(8,128)(2,1)S(1)}, u32[]{:S(2)}, u32[]{:S(2)}) collective-permute-start(bf16[16,256]{1,0:T(8,128)(2,1)S(1)} %collective-permute-done.20), channel_id=1, source_target_pairs={{0,1},{1,2},{2,3},{3,4},{4,5},{5,6},{6,7},{7,8},{8,9},{9,10},{10,1... | collective-permute-start | bytes 24584 | tf_op jit(solution)/shard_map/ppermute | solution.py:27
  302.9 5.8 %collective-permute-start.22 = (bf16[16,256]{1,0:T(8,128)(2,1)S(1)}, bf16[16,256]{1,0:T(8,128)(2,1)S(1)}, u32[]{:S(2)}, u32[]{:S(2)}) collective-permute-start(bf16[16,256]{1,0:T(8,128)(2,1)S(1)} %collective-permute-done.21), channel_id=1, source_target_pairs={{0,1},{1,2},{2,3},{3,4},{4,5},{5,6},{6,7},{7,8},{8,9},{9,10},{10,1... | collective-permute-start | bytes 24584 | tf_op jit(solution)/shard_map/ppermute | solution.py:27
  308.7 5.8 %collective-permute-start.23 = (bf16[16,256]{1,0:T(8,128)(2,1)S(1)}, bf16[16,256]{1,0:T(8,128)(2,1)S(1)}, u32[]{:S(2)}, u32[]{:S(2)}) collective-permute-start(bf16[16,256]{1,0:T(8,128)(2,1)S(1)} %collective-permute-done.22), channel_id=1, source_target_pairs={{0,1},{1,2},{2,3},{3,4},{4,5},{5,6},{6,7},{7,8},{8,9},{9,10},{10,1... | collective-permute-start | bytes 24584 | tf_op jit(solution)/shard_map/ppermute | solution.py:27
  314.5 5.8 %collective-permute-start.24 = (bf16[16,256]{1,0:T(8,128)(2,1)S(1)}, bf16[16,256]{1,0:T(8,128)(2,1)S(1)}, u32[]{:S(2)}, u32[]{:S(2)}) collective-permute-start(bf16[16,256]{1,0:T(8,128)(2,1)S(1)} %collective-permute-done.23), channel_id=1, source_target_pairs={{0,1},{1,2},{2,3},{3,4},{4,5},{5,6},{6,7},{7,8},{8,9},{9,10},{10,1... | collective-permute-start | bytes 24584 | tf_op jit(solution)/shard_map/ppermute | solution.py:27
  357.9 159.5 %reduce-scatter.5.cloned.1.call-start = ((), (), s32[]{:S(2)}) async-start(), calls=%async_computation.3 | async-start | bytes 278528 | tf_op jit(solution)/shard_map/reduce_scatter | solution.py:153
  (25 other events, 131.5 us)
Sparse Core Ops, SparseCore 0:
  99.6 92.9 all-reduce.11
  196.1 53.4 reduce-scatter.2
  358.0 92.4 all-reduce.9
  453.9 53.6 reduce-scatter.4
